TPU v7x, 32 devices: a whole 2x2x4 slice. The times are simulated.
32 devices in a mesh: prompt: 2 (over y), tensor: 4 (over z), ctx: 4 (over x, core).
Axes of the slice: x: 2, y: 2, z: 4, core: 2. Of those that a mesh axis runs over, the one named last changes fastest.
Arguments:
- hidden_in: bfloat16 [2048, 8192], P(('prompt', 'ctx', 'tensor')), parts along dimension 0, may hold values from -6 to 6
- norm_gain: float32 [8192], replicated, may hold values from 0.1 to 1.9
- weight_in: bfloat16 [8192, 3, 4096], P('ctx', None, 'tensor'), may hold values from -0.0625 to 0.0625
- filter_taps: float32 [256, 128], P('tensor'), may hold values from -0.6 to 0.6
- filter_decay: float32 [256], P('tensor'), may hold values from 0.003 to 0.3
- skip_gain: float32 [4096], P('tensor'), may hold values from -1 to 1
- tail_cache: bfloat16 [254, 4096], P('prompt', 'tensor'), parts along dimension 0, may hold values from -6 to 6
- output_weight: bfloat16 [4096, 8192], P(None, 'tensor'), may hold values from -0.09375 to 0.09375
Outputs:
- mixer_output: bfloat16 [2048, 8192], P(('prompt', 'ctx'), 'tensor'), parts along dimension 0
There are 2 independent parts, one for each index of `prompt`. A program takes and returns all parts, laid end to end along the dimension named above; an argument that names none is the same for every part. Nothing has to cross between parts.
All inputs are finite; a program needn't handle non-finite values.
Results may differ from a plain program's by a relative error of at most 0.0095.
Values may be sent and summed in bfloat16 or wider, within the bound.
A program may use at most 256 MiB of HBM per device.

v0:
```python
import jax
import jax.numpy as jnp
from jax import lax
from jax.sharding import PartitionSpec as P

GROUP = 16


def passed_along(value, axis, steps):
    count = lax.axis_size(axis)
    leading, last = (max(0, -steps), min(count, count - steps))
    return lax.ppermute(value, axis, [(source, source + steps) for source in range(leading, last)])


def normalize_rows(hidden_in, norm_gain):
    values = hidden_in.astype(jnp.float32)
    scaled = lax.rsqrt(jnp.mean(values * values, axis=-1, keepdims=True) + 1e-06)
    return (values * scaled * norm_gain[None, :]).astype(jnp.bfloat16)


def banded_taps(taps_full, shard_rows):
    group_count, tap_count = taps_full.shape
    width = shard_rows + tap_count - 1
    first_row = jnp.concatenate(
        [taps_full[:, ::-1], jnp.zeros((group_count, width + 1 - tap_count), jnp.float32)], axis=1
    )
    repeated = jnp.tile(first_row, (1, shard_rows))
    return repeated[:, : shard_rows * width].reshape(group_count, shard_rows, width)


def on_device(
    hidden_in, norm_gain, weight_in, filter_taps, filter_decay, skip_gain, tail_cache, output_weight
):
    gathered = lax.all_gather(hidden_in, "tensor", axis=0, tiled=True)
    normed = normalize_rows(gathered, norm_gain)
    shard_rows = normed.shape[0]
    channels = weight_in.shape[2]
    qkv = jnp.einsum(
        "td,dgc->tgc",
        normed,
        lax.all_gather(weight_in, "ctx", axis=0, tiled=True),
        preferred_element_type=jnp.float32,
    )
    query = qkv[:, 0]
    product = (qkv[:, 1] * qkv[:, 2]).astype(jnp.bfloat16)
    tail_rows = filter_taps.shape[1] - 1
    incoming = passed_along(product[shard_rows - tail_rows :], "ctx", 1)
    leading = lax.axis_index("ctx") == 0
    before = jnp.where(leading, tail_cache, incoming)
    extended = jnp.concatenate([before, product], axis=0).astype(jnp.float32)
    lags = jnp.arange(filter_taps.shape[1]).astype(jnp.float32)
    taps_full = filter_taps * jnp.exp(-filter_decay[:, None] * lags[None, :])
    band = banded_taps(taps_full, shard_rows)
    group_count = taps_full.shape[0]
    grouped = extended.reshape(extended.shape[0], group_count, GROUP)
    filtered = jnp.einsum(
        "gsj,jgi->sgi",
        band,
        grouped,
        precision=lax.Precision.HIGHEST,
        preferred_element_type=jnp.float32,
    ).reshape(shard_rows, channels)
    gated = (query * (filtered + skip_gain[None, :] * product.astype(jnp.float32))).astype(
        jnp.bfloat16
    )
    totals = jnp.dot(
        lax.all_gather(gated, "tensor", axis=1, tiled=True),
        output_weight,
        preferred_element_type=jnp.float32,
    )
    return totals.astype(jnp.bfloat16)


def solution(mesh):
    in_specs = (
        P(("prompt", "ctx", "tensor"), None),
        P(),
        P("ctx", None, "tensor"),
        P("tensor", None),
        P("tensor"),
        P("tensor"),
        P("prompt", "tensor"),
        P(None, "tensor"),
    )
    out_specs = P(("prompt", "ctx"), "tensor")
    return jax.shard_map(
        on_device, mesh=mesh, in_specs=in_specs, out_specs=out_specs, check_vma=False
    )
```

profile of v0, /device:TPU:0, one launch (start us, length us, event | category | flops | bytes accessed | tf_op | source)
XLA Modules:
  0.0 509.6 jit_solution(4066531910178312621)
XLA Ops:
  6.5 0.0 copy-start.4
  6.5 0.0 copy-start.1
  6.5 0.0 all-gather.4.cloned.1.call-start
  6.5 0.7 all-gather.4.cloned.1.call-update
  7.3 0.0 all-gather.6.cloned.1.call-start
  7.3 0.7 all-gather.6.cloned.1.call-update
  8.0 0.0 all-gather.8.cloned.1.call-start
  8.1 0.0 copy-done.4
  8.1 0.0 copy-done.1
  8.1 0.1 exponential_multiply_fusion
  8.2 0.1 rev.3
  8.3 10.3 %tile.4 = f32[64,256,384]{2,1,0:T(8,128)} broadcast(f32[64,384]{1,0:T(8,128)S(1)} %concatenate.7), dimensions={0,2} | broadcast | bytes 25264128 | tf_op jit(solution)/shard_map/tile | solution.py:27
  18.6 22.1 %copy.13 = f32[8,8,256,384]{3,1,2,0:T(8,128)S(1)} copy(f32[8,8,256,384]{3,2,1,0:T(8,128)} %bitcast.25) | data formatting | bytes 50331648
  40.7 8.6 %slice.28 = f32[64,98048]{1,0:T(8,128)} slice(f32[64,98304]{1,0:T(8,128)S(1)} %bitcast.26), slice={[0:64], [0:98048]} | slice | bytes 50200576 | tf_op jit(solution)/shard_map/slice | solution.py:28
  49.3 0.0 copy-start.3
  49.3 32.8 %reshape.33 = f32[64,256,383]{2,1,0:T(8,128)} reshape(f32[64,98048]{1,0:T(8,128)} %slice.28) | data formatting | bytes 50200576 | tf_op jit(solution)/shard_map/reshape | solution.py:28
  82.1 10.3 %all-gather.4.cloned.1.call-done = bf16[256,8192]{1,0:T(8,128)(2,1)} async-done(((bf16[64,8192]{1,0:T(8,128)(2,1)}), bf16[256,8192]{1,0:T(8,128)(2,1)}) %all-gather.4.cloned.1.call-update) | async-done | bytes 4194320 | tf_op jit(solution)/shard_map/all_gather | solution.py:34
  92.4 3.1 fusion
  95.5 0.0 copy-start
  95.5 294.1 %all-gather.6.cloned.1.call-done = bf16[8192,3,1024]{2,0,1:T(8,128)(2,1)} async-done(((bf16[2048,3,1024]{2,0,1:T(8,128)(2,1)}), bf16[8192,3,1024]{2,0,1:T(8,128)(2,1)}) %all-gather.6.cloned.1.call-update) | async-done | bytes 50331664 | tf_op jit(solution)/shard_map/all_gather | solution.py:41
  389.7 0.0 copy-done.3
  389.7 21.9 %fusion.4 = f32[256,3,1024]{2,0,1:T(8,128)S(1)} fusion(bf16[8192,3,1024]{2,0,1:T(8,128)(2,1)} %all-gather.6.cloned.1.call-done, bf16[256,8192]{1,0:T(8,128)(2,1)} %all-gather.4.cloned.1.call-done, f32[8192]{0:T(1024)S(1)} %copy-done.3, f32[256]{0:T(256)S(1)} %add_rsqrt_fusion), kind=kOutput, calls=%fused_computation.6 | convolution fusion | flops 12893290496 | bytes 57705472 | tf_op jit(solution)/shard_map/td,dgc->tgc/dot_general | solution.py:38
  411.6 0.1 fusion.8
  411.8 0.1 slice_bitcast_fusion.1
  411.8 2.4 collective-permute-start
  414.2 0.1 fusion.17
  414.3 0.8 collective-permute-done
  415.1 0.0 copy-done
  415.2 1.0 pad_maximum_fusion
  416.2 2.3 copy.11
  418.5 0.0 copy-start.2
  418.5 17.3 %fusion.11 = f32[64,16,256]{2,1,0:T(8,128)} fusion(bf16[383,64,16]{0,2,1:T(8,128)(2,1)} %bitcast.28, f32[64,256,383]{2,1,0:T(8,128)} %reshape.33), kind=kOutput, calls=%fused_computation.21 | convolution fusion | flops 1204813824 | bytes 26933248 | tf_op jit(solution)/shard_map/gsj,jgi->sgi/dot_general | solution.py:56
  435.8 2.5 copy.12
  438.3 0.0 copy-done.2
  438.3 2.4 fusion.10
  440.7 0.0 all-gather.8.cloned.1.call-update
  440.8 50.5 %all-gather.8.cloned.1.call-done = bf16[256,4096]{1,0:T(8,128)(2,1)} async-done(((bf16[256,1024]{1,0:T(8,128)(2,1)}), bf16[256,4096]{1,0:T(8,128)(2,1)}) %all-gather.8.cloned.1.call-update) | async-done | bytes 2097168 | tf_op jit(solution)/shard_map/all_gather | solution.py:67
  491.2 11.9 %convolution_convert_fusion = bf16[256,2048]{1,0:T(8,128)(2,1)} fusion(bf16[256,4096]{1,0:T(8,128)(2,1)} %all-gather.8.cloned.1.call-done, bf16[4096,2048]{1,0:T(8,128)(2,1)} %param.15), kind=kOutput, calls=%fused_computation.9 | convolution fusion | flops 4295491584 | bytes 19922944 | tf_op jit(solution)/shard_map/dot_general | solution.py:66
  (5 shorter events, 0.1 us)
Async XLA Ops:
  6.5 1.5 copy-start.4
  6.5 1.6 copy-start.1
  6.5 85.9 %all-gather.4.cloned.1.call-start = ((), (), s32[]{:S(2)}) async-start(), calls=%async_computation | async-start | bytes 5242880 | tf_op jit(solution)/shard_map/all_gather | solution.py:34
  7.3 382.4 %all-gather.6.cloned.1.call-start = ((), (), s32[]{:S(2)}) async-start(), calls=%async_computation.1 | async-start | bytes 62914560 | tf_op jit(solution)/shard_map/all_gather | solution.py:41
  8.0 483.2 %all-gather.8.cloned.1.call-start = ((), (), s32[]{:S(2)}) async-start(), calls=%async_computation.2 | async-start | bytes 2621440 | tf_op jit(solution)/shard_map/all_gather | solution.py:67
  49.3 340.4 %copy-start.3 = (f32[8192]{0:T(1024)S(1)}, f32[8192]{0:T(1024)}, u32[]{:S(2)}) copy-start(f32[8192]{0:T(1024)} %param.9) | copy-start | bytes 98308
  95.5 319.6 %copy-start = (bf16[127,1024]{1,0:T(8,128)(2,1)S(1)}, bf16[127,1024]{1,0:T(8,128)(2,1)}, u32[]{:S(2)}) copy-start(bf16[127,1024]{1,0:T(8,128)(2,1)} %param.14) | copy-start | bytes 780292
  411.8 3.3 collective-permute-start
  418.5 19.8 %copy-start.2 = (f32[1024]{0:T(1024)S(1)}, f32[1024]{0:T(1024)}, u32[]{:S(2)}) copy-start(f32[1024]{0:T(1024)} %param.13) | copy-start | bytes 12292
Sparse Core Ops, SparseCore 0:
  8.9 83.4 all-gather.3
  94.0 295.6 all-gather.5
  440.9 50.3 all-gather.7
where the time goes:
time: 510 us
  waiting for transfers between devices  357 us (70%)
  local copies, waits for them, and re-layouts  78.8 us (15%)
  matrix products  51.1 us (10%)
  between operations  13.2 us (3%)
  other arithmetic  6.97 us (1%)
    all_gather x1, waiting for transfers between devices, on_device(): lax.all_gather(weight_in, 'ctx', axis=0, tiled=True)  294 us
    all_gather x1, waiting for transfers between devices, on_device(): lax.all_gather(gated, 'tensor', axis=1, tiled=True)  50.5 us
    reshape x1, local copies, waits for them, and re-layouts, banded_taps(): repeated[:, :shard_rows * width].reshape(group_count, shard_rows, width)  32.8 us
    unnamed x11, local copies, waits for them, and re-layouts  22.1 us
    dot_general x1, matrix products, on_device(): jnp.einsum('td,dgc->tgc', normed, lax.all_gather(weight_in, 'ctx', axis=0...  21.9 us
    dot_general x1, matrix products, on_device(): jnp.einsum('gsj,jgi->sgi', band, grouped, precision=lax.Precision.HIGHEST...  17.3 us
    dot_general x1, matrix products, on_device(): jnp.dot(lax.all_gather(gated, 'tensor', axis=1, tiled=True), output_weigh...  11.9 us
    another operation x1, local copies, waits for them, and re-layouts, banded_taps(): repeated = jnp.tile(first_row, (1, shard_rows))  10.3 us
  transfers between devices with their start and end apart: 4, of which 4 were waited for; matrix products, arithmetic and copies ran while one was open for 15% of the time, Pallas kernels for 0%

commit v1 on v0

v1 whole, which is shorter than its diff:
```python
import jax
import jax.numpy as jnp
from jax import lax
from jax.experimental import pallas as pl
from jax.experimental.pallas import tpu as pltpu
from jax.sharding import PartitionSpec as P

GROUP = 16
LANES = 128


def passed_along(value, axis, steps):
    count = lax.axis_size(axis)
    leading, last = (max(0, -steps), min(count, count - steps))
    return lax.ppermute(value, axis, [(source, source + steps) for source in range(leading, last)])


def normalize_rows(hidden_in, norm_gain):
    values = hidden_in.astype(jnp.float32)
    scaled = lax.rsqrt(jnp.mean(values * values, axis=-1, keepdims=True) + 1e-06)
    return (values * scaled * norm_gain[None, :]).astype(jnp.bfloat16)


def toeplitz_kernel(rows_ref, bands_ref):
    for group in range(bands_ref.shape[0]):
        row = jnp.broadcast_to(rows_ref[group : group + 1, :], bands_ref.shape[1:])
        bands_ref[group] = pltpu.roll(row, 0, 1, stride=1, stride_axis=0).astype(jnp.bfloat16)


def banded_taps(filter_taps, filter_decay):
    groups, tap_count = filter_taps.shape
    lags = jnp.arange(tap_count).astype(jnp.float32)
    taps_full = filter_taps * jnp.exp(-filter_decay[:, None] * lags[None, :])
    rows = jnp.concatenate(
        [
            jnp.zeros((groups, 1), jnp.float32),
            taps_full[:, ::-1],
            jnp.zeros((groups, tap_count - 1), jnp.float32),
        ],
        axis=1,
    )
    block = 8
    return pl.pallas_call(
        toeplitz_kernel,
        grid=(groups // block,),
        in_specs=[pl.BlockSpec((block, 2 * tap_count), lambda i: (i, 0))],
        out_specs=pl.BlockSpec((block, tap_count, 2 * tap_count), lambda i: (i, 0, 0)),
        out_shape=jax.ShapeDtypeStruct((groups, tap_count, 2 * tap_count), jnp.bfloat16),
        cost_estimate=pl.CostEstimate(
            flops=groups * tap_count * tap_count * 16,
            bytes_accessed=groups * tap_count * tap_count * 4,
            transcendentals=0,
        ),
    )(rows)


def filter_kernel(query_ref, before_ref, product_ref, skip_ref, bands_ref, gated_ref):
    taps = bands_ref.shape[1]
    rows = product_ref.shape[0]
    blocks = rows // taps
    extended = jnp.concatenate([before_ref[...], product_ref[...]], axis=0)
    windows = jnp.concatenate(
        [extended[b * taps : (b + 2) * taps] for b in range(blocks)], axis=1
    )
    lane = lax.broadcasted_iota(jnp.int32, windows.shape, 1)
    owner = lax.rem(lane, LANES) // GROUP
    total = jnp.zeros((taps, blocks * LANES), jnp.float32)
    for group in range(LANES // GROUP):
        own = jnp.where(owner == group, windows, jnp.zeros_like(windows))
        total = total + jnp.dot(bands_ref[group], own, preferred_element_type=jnp.float32)
    for b in range(blocks):
        span = pl.ds(b * taps, taps)
        filtered = total[:, b * LANES : (b + 1) * LANES]
        product = product_ref[span, :].astype(jnp.float32)
        query = query_ref[span, :].astype(jnp.float32)
        gated_ref[span, :] = (query * (filtered + skip_ref[...] * product)).astype(jnp.bfloat16)


def filtered_and_gated(query, before, product, skip_gain, bands):
    rows, channels = product.shape
    taps = bands.shape[1]
    per = LANES // GROUP
    column = lambda i: (0, i)
    return pl.pallas_call(
        filter_kernel,
        grid=(channels // LANES,),
        in_specs=[
            pl.BlockSpec((rows, LANES), column),
            pl.BlockSpec((taps, LANES), column),
            pl.BlockSpec((rows, LANES), column),
            pl.BlockSpec((1, LANES), column),
            pl.BlockSpec((per, taps, 2 * taps), lambda i: (i, 0, 0)),
        ],
        out_specs=pl.BlockSpec((rows, LANES), column),
        out_shape=jax.ShapeDtypeStruct((rows, channels), jnp.bfloat16),
    )(query, before, product, skip_gain.reshape(1, channels), bands)


def on_device(
    hidden_in, norm_gain, weight_in, filter_taps, filter_decay, skip_gain, tail_cache, output_weight
):
    rows, width = hidden_in.shape
    depth, _, channels = weight_in.shape
    taps = filter_taps.shape[1]
    normed = normalize_rows(hidden_in, norm_gain)
    parts = width // depth
    pieces = jnp.stack([normed[:, p * depth : (p + 1) * depth] for p in range(parts)])
    pieces = lax.all_to_all(pieces, "ctx", 0, 0, tiled=True)
    pieces = lax.all_gather(pieces, "tensor", axis=0)
    pieces = pieces.transpose(1, 0, 2, 3)
    shards = pieces.shape[1]
    pieces = pieces.reshape(parts * shards * rows, depth)
    planes = weight_in.transpose(1, 0, 2)

    def projected(which):
        partial = jnp.dot(pieces, planes[which], preferred_element_type=jnp.float32)
        return lax.psum_scatter(
            partial.astype(jnp.bfloat16), "ctx", scatter_dimension=0, tiled=True
        )

    key, value, query = (projected(which) for which in (1, 2, 0))
    product = (key.astype(jnp.float32) * value.astype(jnp.float32)).astype(jnp.bfloat16)
    incoming = passed_along(product[product.shape[0] - taps :], "ctx", 1)
    leading = lax.axis_index("ctx") == 0
    tail = jnp.concatenate([jnp.zeros((1, channels), jnp.bfloat16), tail_cache], axis=0)
    before = jnp.where(leading, tail, incoming)
    bands = banded_taps(filter_taps, filter_decay)
    gated = filtered_and_gated(query, before, product, skip_gain, bands)
    totals = jnp.dot(
        lax.all_gather(gated, "tensor", axis=1, tiled=True),
        output_weight,
        preferred_element_type=jnp.float32,
    )
    return totals.astype(jnp.bfloat16)


def solution(mesh):
    in_specs = (
        P(("prompt", "ctx", "tensor"), None),
        P(),
        P("ctx", None, "tensor"),
        P("tensor", None),
        P("tensor"),
        P("tensor"),
        P("prompt", "tensor"),
        P(None, "tensor"),
    )
    out_specs = P(("prompt", "ctx"), "tensor")
    return jax.shard_map(
        on_device, mesh=mesh, in_specs=in_specs, out_specs=out_specs, check_vma=False
    )
```

time: 510 us -> 293 us (0.57)
  waiting for transfers between devices: 357 us -> 196 us
  local copies, waits for them, and re-layouts: 78.8 us -> 4.7 us
  blocking collectives: 0 us -> 18.6 us
  Pallas kernels: 0 us -> 12.8 us
  matrix products: 51.1 us -> 38.4 us
    all_gather x2 -> x1, waiting for transfers between devices: 304 us -> 81.7 us  [on_device(): pieces = lax.all_gather(pieces, 'tensor', axis=0)]
    reduce_scatter x0 -> x3, waiting for transfers between devices: none -> 68.6 us  [projected(): lax.psum_scatter(partial.astype(jnp.bfloat16), 'ctx', scatter_dimension=0...]
    reshape x2 -> x0, local copies, waits for them, and re-layouts: 35.4 us -> none  [the longest x1 32.8 us: banded_taps(): repeated[:, :shard_rows * width].reshape(group_count, shard_rows, width)]
    unnamed x11 -> x10, local copies, waits for them, and re-layouts: 22.1 us -> 1.96 us
    all_to_all x0 -> x1, blocking collectives: none -> 18.6 us  [on_device(): pieces = lax.all_to_all(pieces, 'ctx', 0, 0, tiled=True)]
    pallas_call x0 -> x2, Pallas kernels: none -> 12.8 us  [the longest x1 7.33 us: filtered_and_gated(): pl.pallas_call(filter_kernel, grid=(channels // LANES,), in_specs=[pl.Blo...]
    dot_general x2 -> x3, matrix products: 39.2 us -> 26.5 us  [projected(): partial = jnp.dot(pieces, planes[which], preferred_element_type=jnp.float32)]
    another operation x1, local copies, waits for them, and re-layouts: 10.3 us -> 0.07 us  [on_device(): jnp.stack([normed[:, p * depth:(p + 1) * depth] for p in range(parts)])]
  transfers between devices with their start and end apart: 4 -> 6, of which waited for: 4 -> 5; matrix products, arithmetic and copies ran while one was open for 15% -> 7% of each run, Pallas kernels for 0% -> 2%
where the time goes in v1:
time: 293 us
  waiting for transfers between devices  196 us (67%)
  matrix products  38.4 us (13%)
  blocking collectives  18.6 us (6%)
  between operations  13.3 us (5%)
  Pallas kernels  12.8 us (4%)
  other arithmetic  6.22 us (2%)
  local copies, waits for them, and re-layouts  4.7 us (2%)
    all_gather x1, waiting for transfers between devices, on_device(): pieces = lax.all_gather(pieces, 'tensor', axis=0)  81.7 us
    reduce_scatter x3, waiting for transfers between devices, projected(): lax.psum_scatter(partial.astype(jnp.bfloat16), 'ctx', scatter_dimension=0...  68.6 us
    all_gather x1, waiting for transfers between devices, on_device(): lax.all_gather(gated, 'tensor', axis=1, tiled=True)  46.1 us
    dot_general x3, matrix products, projected(): partial = jnp.dot(pieces, planes[which], preferred_element_type=jnp.float32)  26.5 us
    all_to_all x1, blocking collectives, on_device(): pieces = lax.all_to_all(pieces, 'ctx', 0, 0, tiled=True)  18.6 us
    dot_general x1, matrix products, on_device(): jnp.dot(lax.all_gather(gated, 'tensor', axis=1, tiled=True), output_weigh...  11.9 us
    pallas_call x1, Pallas kernels, filtered_and_gated(): pl.pallas_call(filter_kernel, grid=(channels // LANES,), in_specs=[pl.Blo...  7.33 us
  transfers between devices with their start and end apart: 6, of which 5 were waited for; matrix products, arithmetic and copies ran while one was open for 7% of the time, Pallas kernels for 2%

profile of v1, /device:TPU:0, one launch (start us, length us, event | category | flops | bytes accessed | tf_op | source)
XLA Modules:
  0.0 292.6 jit_solution(5884215739928871377)
XLA Ops:
  6.5 0.0 all-gather.6.cloned.1.call-start
  6.5 1.5 fusion.3
  8.1 1.5 fusion.5
  9.6 0.1 slice_bitcast_fusion.15
  9.7 0.1 pad_maximum_fusion
  9.8 18.6 %all_to_all.5 = bf16[4,64,2048]{2,1,0:T(8,128)(2,1)} all-to-all(bf16[4,64,2048]{2,1,0:T(8,128)(2,1)S(1)} %pad_maximum_fusion), channel_id=1, replica_groups=mesh['prompt'=2,'tensor'=4,'ctx'=4] {'ctx'}, dimensions={0} | all-to-all | bytes 2097152 | tf_op jit(solution)/shard_map/all_to_all | solution.py:108
  28.4 0.0 all-gather.6.cloned.1.call-update
  28.5 0.0 reduce-scatter.6.cloned.1.call-start
  28.5 81.7 %all-gather.6.cloned.1.call-done = bf16[16,64,2048]{2,1,0:T(8,128)(2,1)} async-done(((bf16[4,64,2048]{2,1,0:T(8,128)(2,1)}), bf16[16,64,2048]{2,1,0:T(8,128)(2,1)}) %all-gather.6.cloned.1.call-update) | async-done | bytes 4194320 | tf_op jit(solution)/shard_map/all_gather | solution.py:109
  110.2 2.5 copy.10
  112.7 0.0 copy-start
  112.7 1.9 copy-done
  114.6 7.9 %fusion.7 = bf16[1024,1024]{1,0:T(8,128)(2,1)} fusion(bf16[1024,2048]{1,0:T(8,128)(2,1)S(1)} %bitcast.35, bf16[3,2048,1024]{2,1,0:T(8,128)(2,1)} %bitcast.40), kind=kOutput, calls=%fused_computation.13 | convolution fusion | flops 4296015872 | bytes 10485760 | tf_op jit(solution)/shard_map/dot_general | solution.py:116
  122.5 0.0 reduce-scatter.6.cloned.1.call-update
  122.6 0.0 reduce-scatter.8.cloned.1.call-start
  122.6 9.3 %fusion.8 = bf16[1024,1024]{1,0:T(8,128)(2,1)} fusion(bf16[1024,2048]{1,0:T(8,128)(2,1)} %bitcast.36, bf16[3,2048,1024]{2,1,0:T(8,128)(2,1)} %bitcast.41), kind=kOutput, calls=%fused_computation.14 | convolution fusion | flops 4296015872 | bytes 10485760 | tf_op jit(solution)/shard_map/dot_general | solution.py:116
  131.9 0.0 reduce-scatter.8.cloned.1.call-update
  132.0 0.0 copy-start.4
  132.0 0.0 reduce-scatter.4.cloned.1.call-start
  132.0 9.3 %fusion.6 = bf16[1024,1024]{1,0:T(8,128)(2,1)} fusion(bf16[1024,2048]{1,0:T(8,128)(2,1)} %bitcast.37, bf16[3,2048,1024]{2,1,0:T(8,128)(2,1)} %bitcast.42), kind=kOutput, calls=%fused_computation.12 | convolution fusion | flops 4296015872 | bytes 10485760 | tf_op jit(solution)/shard_map/dot_general | solution.py:116
  141.3 0.0 copy-start.3
  141.3 0.0 copy-start.2
  141.3 0.0 reduce-scatter.4.cloned.1.call-update
  141.3 0.0 all-gather.4.cloned.1.call-start
  141.4 0.0 copy-done.4
  141.4 11.3 %reduce-scatter.6.cloned.1.call-done = bf16[256,1024]{1,0:T(8,128)(2,1)} async-done(((bf16[1024,1024]{1,0:T(8,128)(2,1)}), bf16[256,1024]{1,0:T(8,128)(2,1)}) %reduce-scatter.6.cloned.1.call-update) | async-done | bytes 524304 | tf_op jit(solution)/shard_map/reduce_scatter | solution.py:117
  152.7 34.2 %reduce-scatter.8.cloned.1.call-done = bf16[256,1024]{1,0:T(8,128)(2,1)} async-done(((bf16[1024,1024]{1,0:T(8,128)(2,1)}), bf16[256,1024]{1,0:T(8,128)(2,1)}) %reduce-scatter.8.cloned.1.call-update) | async-done | bytes 524304 | tf_op jit(solution)/shard_map/reduce_scatter | solution.py:117
  186.8 1.4 multiply_convert_fusion.product_ref
  188.2 0.0 copy-start.1
  188.3 1.9 collective-permute-start
  190.2 0.0 copy-done.3
  190.2 0.1 exponential_multiply_fusion
  190.3 0.1 rev.3
  190.4 0.1 pad.3.clone
  190.5 0.7 maximum_maximum_fusion.rows_ref
  191.2 5.5 %shard_map.82.bands_ref = bf16[64,128,256]{2,1,0:T(8,128)(2,1)} custom-call(f32[64,256]{1,0:T(8,128)} %maximum_maximum_fusion.rows_ref), custom_call_target="tpu_custom_call" | custom-call | flops 16777216 | bytes 4194304 | tf_op jit(solution)/shard_map/pallas_call | solution.py:43
  196.7 0.0 collective-permute-done
  196.7 0.0 copy-done.2
  196.7 0.8 pad_select_fusion.before_ref
  197.5 23.2 %reduce-scatter.4.cloned.1.call-done.query_ref = bf16[256,1024]{1,0:T(8,128)(2,1)} async-done(((bf16[1024,1024]{1,0:T(8,128)(2,1)}), bf16[256,1024]{1,0:T(8,128)(2,1)}) %reduce-scatter.4.cloned.1.call-update) | async-done | bytes 524304 | tf_op jit(solution)/shard_map/reduce_scatter | solution.py:117
  220.7 0.0 copy-done.1
  220.7 7.3 %shard_map.83 = bf16[256,1024]{1,0:T(8,128)(2,1)} custom-call(bf16[256,1024]{1,0:T(8,128)(2,1)} %reduce-scatter.4.cloned.1.call-done.query_ref, bf16[128,1024]{1,0:T(8,128)(2,1)} %pad_select_fusion.before_ref, bf16[256,1024]{1,0:T(8,128)(2,1)} %copy-done.1, f32[1,1024]{1,0:T(1,128)} %bitcast.39, bf16[64,128,256]{2,1,0:T(8,128)(2,1)} %shard_map.82.bands_ref), custom_call_target="tpu_custom_call" | custom-call | tf_op jit(solution)/shard_map/pallas_call | solution.py:84
  228.0 0.0 all-gather.4.cloned.1.call-update
  228.1 46.1 %all-gather.4.cloned.1.call-done = bf16[256,4096]{1,0:T(8,128)(2,1)} async-done(((bf16[256,1024]{1,0:T(8,128)(2,1)}), bf16[256,4096]{1,0:T(8,128)(2,1)}) %all-gather.4.cloned.1.call-update) | async-done | bytes 2097168 | tf_op jit(solution)/shard_map/all_gather | solution.py:130
  274.2 11.9 %convolution_convert_fusion = bf16[256,2048]{1,0:T(8,128)(2,1)} fusion(bf16[256,4096]{1,0:T(8,128)(2,1)} %all-gather.4.cloned.1.call-done, bf16[4096,2048]{1,0:T(8,128)(2,1)} %param.15), kind=kOutput, calls=%fused_computation.8 | convolution fusion | flops 4295491584 | bytes 19922944 | tf_op jit(solution)/shard_map/dot_general | solution.py:129
  (6 shorter events, 0.0 us)
Async XLA Ops:
  6.5 103.6 %all-gather.6.cloned.1.call-start = ((), (), s32[]{:S(2)}) async-start(), calls=%async_computation.8 | async-start | bytes 5242880 | tf_op jit(solution)/shard_map/all_gather | solution.py:109
  28.5 124.2 %reduce-scatter.6.cloned.1.call-start = ((), (), s32[]{:S(2)}) async-start(), calls=%async_computation.5 | async-start | bytes 2621440 | tf_op jit(solution)/shard_map/reduce_scatter | solution.py:117
  112.7 1.9 copy-start
  122.6 64.3 %reduce-scatter.8.cloned.1.call-start = ((), (), s32[]{:S(2)}) async-start(), calls=%async_computation.6 | async-start | bytes 2621440 | tf_op jit(solution)/shard_map/reduce_scatter | solution.py:117
  132.0 9.4 %copy-start.4 = (f32[64]{0:T(128)S(1)}, f32[64]{0:T(128)}, u32[]{:S(2)}) copy-start(f32[64]{0:T(128)} %param.12) | copy-start | bytes 772
  132.0 88.7 %reduce-scatter.4.cloned.1.call-start = ((), (), s32[]{:S(2)}) async-start(), calls=%async_computation.4 | async-start | bytes 2621440 | tf_op jit(solution)/shard_map/reduce_scatter | solution.py:117
  141.3 48.9 %copy-start.3 = (f32[64,128]{1,0:T(8,128)S(1)}, f32[64,128]{1,0:T(8,128)}, u32[]{:S(2)}) copy-start(f32[64,128]{1,0:T(8,128)} %param.11) | copy-start | bytes 98308
  141.3 55.4 %copy-start.2 = (bf16[127,1024]{1,0:T(8,128)(2,1)S(1)}, bf16[127,1024]{1,0:T(8,128)(2,1)}, u32[]{:S(2)}) copy-start(bf16[127,1024]{1,0:T(8,128)(2,1)} %param.14) | copy-start | bytes 780292
  141.3 132.8 %all-gather.4.cloned.1.call-start = ((), (), s32[]{:S(2)}) async-start(), calls=%async_computation.7 | async-start | bytes 2621440 | tf_op jit(solution)/shard_map/all_gather | solution.py:130
  188.2 32.5 %copy-start.1 = (bf16[256,1024]{1,0:T(8,128)(2,1)}, bf16[256,1024]{1,0:T(8,128)(2,1)S(1)}, u32[]{:S(2)}) copy-start(bf16[256,1024]{1,0:T(8,128)(2,1)S(1)} %multiply_convert_fusion.product_ref) | copy-start | bytes 1572868
  188.3 8.4 %collective-permute-start = (bf16[128,1024]{1,0:T(8,128)(2,1)S(1)}, bf16[128,1024]{1,0:T(8,128)(2,1)S(1)}, u32[]{:S(2)}, u32[]{:S(2)}) collective-permute-start(bf16[128,1024]{1,0:T(8,128)(2,1)S(1)} %slice.39), channel_id=1, source_target_pairs={{0,1},{1,2},{2,3},{4,5},{5,6},{6,7},{8,9},{9,10},{10,11},{12,13},{... | collective-permute-start | bytes 786440 | tf_op jit(solution)/shard_map/ppermute | solution.py:15
Sparse Core Ops, SparseCore 0:
  28.6 81.5 all-gather.5
  122.7 29.9 reduce-scatter.5
  155.4 31.4 reduce-scatter.7
  189.2 31.4 reduce-scatter.3
  228.2 45.9 all-gather.3

commit v2 on v1

--- a/solution.py
+++ b/solution.py
@@ -1,3 +1,4 @@
+import functools
 import jax
 import jax.numpy as jnp
 from jax import lax
@@ -96,42 +97,319 @@
     )(query, before, product, skip_gain.reshape(1, channels), bands)
 
 
+MESH = pl.DeviceIdType.MESH
+
+
+def greet(axis_peers):
+    barrier = pltpu.get_barrier_semaphore()
+    for axis, peer, there in axis_peers:
+
+        @pl.when(there)
+        def _(axis=axis, peer=peer):
+            pl.semaphore_signal(barrier, inc=1, device_id={axis: peer}, device_id_type=MESH)
+
+    pl.semaphore_wait(barrier, sum(jnp.where(there, 1, 0) for _, _, there in axis_peers))
+
+
+def line_neighbours(count):
+    place = lax.axis_index("tensor")
+    return [
+        ("tensor", jnp.maximum(place - 1, 0), place > 0),
+        ("tensor", jnp.minimum(place + 1, count - 1), place < count - 1),
+    ]
+
+
+def hop(slots, origin, way, send_sem, recv_sem, count):
+    place = lax.axis_index("tensor")
+    target = jnp.clip(place + 2 * way - 1, 0, count - 1)
+    return pltpu.make_async_remote_copy(
+        src_ref=slots.at[origin],
+        dst_ref=slots.at[origin],
+        send_sem=send_sem.at[way, origin],
+        recv_sem=recv_sem.at[origin],
+        device_id={"tensor": target},
+        device_id_type=MESH,
+    )
+
+
+def relay(slots, send_sem, recv_sem, count, use):
+    place = lax.axis_index("tensor")
+
+    def send(origin, way):
+        @pl.when((place + 1 < count) if way else (place > 0))
+        def _():
+            hop(slots, origin, way, send_sem, recv_sem, count).start()
+
+    send(place, 0)
+    send(place, 1)
+    use(place)
+
+    def step(distance, carry):
+        below, above = place - distance, place + distance
+
+        @pl.when(below >= 0)
+        def _():
+            origin = jnp.maximum(below, 0)
+            hop(slots, origin, 1, send_sem, recv_sem, count).wait_recv()
+            send(origin, 1)
+
+        @pl.when(above < count)
+        def _():
+            origin = jnp.minimum(above, count - 1)
+            hop(slots, origin, 0, send_sem, recv_sem, count).wait_recv()
+            send(origin, 0)
+
+        @pl.when(below >= 0)
+        def _():
+            use(jnp.maximum(below, 0))
+
+        @pl.when(above < count)
+        def _():
+            use(jnp.minimum(above, count - 1))
+
+        return carry
+
+    lax.fori_loop(1, count, step, 0)
+
+
+def relay_sent(slots, send_sem, recv_sem, count):
+    place = lax.axis_index("tensor")
+
+    def step(origin, carry):
+        @pl.when((origin <= place) & (place + 1 < count))
+        def _():
+            hop(slots, origin, 1, send_sem, recv_sem, count).wait_send()
+
+        @pl.when((origin >= place) & (place > 0))
+        def _():
+            hop(slots, origin, 0, send_sem, recv_sem, count).wait_send()
+
+        return carry
+
+    lax.fori_loop(0, count, step, 0)
+
+
+def project_kernel(
+    shards,
+    parts,
+    normed_ref,
+    planes_ref,
+    query_ref,
+    product_ref,
+    planes,
+    slots,
+    partial,
+    arrived,
+    load_sem,
+    own_sem,
+    swap_send,
+    swap_recv,
+    line_send,
+    line_recv,
+    sum_send,
+    sum_recv,
+):
+    rows = normed_ref.shape[0]
+    _, depth, channels = planes.shape
+    tile = min(256, channels)
+    me, place = lax.axis_index("ctx"), lax.axis_index("tensor")
+    others = [lax.rem(me + 1 + k, parts) for k in range(parts - 1)]
+    loads = [
+        pltpu.make_async_copy(planes_ref.at[g], planes.at[g], load_sem.at[g]) for g in (1, 2, 0)
+    ]
+    for load in loads:
+        load.start()
+    greet([("ctx", other, me >= 0) for other in others] + line_neighbours(shards))
+
+    def span(index, size):
+        return pl.ds(pl.multiple_of(index * size, size), size)
+
+    swaps = [
+        pltpu.make_async_remote_copy(
+            src_ref=normed_ref.at[:, span(other, depth)],
+            dst_ref=slots.at[place, span(me, rows)],
+            send_sem=swap_send.at[k],
+            recv_sem=swap_recv.at[parts - 2 - k],
+            device_id={"ctx": other},
+            device_id_type=MESH,
+        )
+        for k, other in enumerate(others)
+    ]
+    for swap in swaps:
+        swap.start()
+    own = pltpu.make_async_copy(
+        normed_ref.at[:, span(me, depth)], slots.at[place, span(me, rows)], own_sem
+    )
+    own.start()
+    own.wait()
+    for swap in swaps:
+        swap.wait_recv()
+    for load in loads:
+        load.wait()
+
+    def use(origin):
+        def plane(step, carry):
+            g = lax.rem(step + 1, 3)
+
+            def columns(index, inner):
+                where = span(index, tile)
+                partial[g, origin, :, where] = jnp.dot(
+                    slots[origin], planes[g, :, where], preferred_element_type=jnp.float32
+                ).astype(jnp.bfloat16)
+                return inner
+
+            lax.fori_loop(0, channels // tile, columns, 0)
+            for k, other in enumerate(others):
+                pltpu.make_async_remote_copy(
+                    src_ref=partial.at[g, origin, span(other, rows)],
+                    dst_ref=arrived.at[g, parts - 2 - k, span(origin, rows)],
+                    send_sem=sum_send,
+                    recv_sem=sum_recv.at[g],
+                    device_id={"ctx": other},
+                    device_id_type=MESH,
+                ).start()
+            return carry
+
+        lax.fori_loop(0, 3, plane, 0)
+
+    relay(slots, line_send, line_recv, shards, use)
+
+    def total(g, origin):
+        value = partial[g, origin, span(me, rows)].astype(jnp.float32)
+        for k in range(parts - 1):
+            value = value + arrived[g, k, span(origin, rows)].astype(jnp.float32)
+        return value
+
+    for g in (1, 2):
+        pltpu.make_async_copy(arrived.at[g], arrived.at[g], sum_recv.at[g]).wait()
+
+    def write_product(origin, carry):
+        product_ref[span(origin, rows), :] = (total(1, origin) * total(2, origin)).astype(
+            jnp.bfloat16
+        )
+        return carry
+
+    lax.fori_loop(0, shards, write_product, 0)
+    pltpu.make_async_copy(arrived.at[0], arrived.at[0], sum_recv.at[0]).wait()
+
+    def write_query(origin, carry):
+        query_ref[span(origin, rows), :] = total(0, origin)
+        return carry
+
+    lax.fori_loop(0, shards, write_query, 0)
+    for swap in swaps:
+        swap.wait_send()
+    relay_sent(slots, line_send, line_recv, shards)
+    pltpu.make_async_copy(arrived, arrived, sum_send).wait()
+
+
+def projected(normed, planes):
+    shards, parts = lax.axis_size("tensor"), lax.axis_size("ctx")
+    rows = normed.shape[0]
+    _, depth, channels = planes.shape
+    vmem = pl.BlockSpec(memory_space=pltpu.VMEM)
+    dma = pltpu.SemaphoreType.DMA
+    return pl.pallas_call(
+        functools.partial(project_kernel, shards, parts),
+        out_shape=(
+            jax.ShapeDtypeStruct((shards * rows, channels), jnp.float32),
+            jax.ShapeDtypeStruct((shards * rows, channels), jnp.bfloat16),
+        ),
+        in_specs=[vmem, pl.BlockSpec(memory_space=pl.ANY)],
+        out_specs=(vmem, vmem),
+        scratch_shapes=[
+            pltpu.VMEM((3, depth, channels), jnp.bfloat16),
+            pltpu.VMEM((shards, parts * rows, depth), jnp.bfloat16),
+            pltpu.VMEM((3, shards, parts * rows, channels), jnp.bfloat16),
+            pltpu.VMEM((3, parts - 1, shards * rows, channels), jnp.bfloat16),
+            dma((3,)),
+            dma,
+            dma((parts - 1,)),
+            dma((parts - 1,)),
+            dma((2, shards)),
+            dma((shards,)),
+            dma,
+            dma((3,)),
+        ],
+        compiler_params=pltpu.CompilerParams(
+            collective_id=0, has_side_effects=True, vmem_limit_bytes=44 << 20
+        ),
+    )(normed, planes)
+
+
+def output_kernel(
+    shards, gated_ref, weight_ref, out_ref, weight, slots, total, load_sem, own_sem, line_send, line_recv
+):
+    channels = gated_ref.shape[1]
+    columns = out_ref.shape[1]
+    tile = min(256, columns)
+    place = lax.axis_index("tensor")
+    load = pltpu.make_async_copy(weight_ref, weight, load_sem)
+    load.start()
+    own = pltpu.make_async_copy(gated_ref, slots.at[place], own_sem)
+    own.start()
+    greet(line_neighbours(shards))
+    own.wait()
+    total[...] = jnp.zeros_like(total)
+
+    def use(origin):
+        deep = pl.ds(pl.multiple_of(origin * channels, channels), channels)
+
+        def column(index, carry):
+            where = pl.ds(pl.multiple_of(index * tile, tile), tile)
+            total[:, where] += jnp.dot(
+                slots[origin], weight[deep, where], preferred_element_type=jnp.float32
+            )
+            return carry
+
+        lax.fori_loop(0, columns // tile, column, 0)
+
+    load.wait()
+    relay(slots, line_send, line_recv, shards, use)
+    out_ref[...] = total[...].astype(jnp.bfloat16)
+    relay_sent(slots, line_send, line_recv, shards)
+
+
+def output_projection(gated, output_weight):
+    shards = lax.axis_size("tensor")
+    rows, channels = gated.shape
+    depth, columns = output_weight.shape
+    vmem = pl.BlockSpec(memory_space=pltpu.VMEM)
+    dma = pltpu.SemaphoreType.DMA
+    return pl.pallas_call(
+        functools.partial(output_kernel, shards),
+        out_shape=jax.ShapeDtypeStruct((rows, columns), jnp.bfloat16),
+        in_specs=[vmem, pl.BlockSpec(memory_space=pl.ANY)],
+        out_specs=vmem,
+        scratch_shapes=[
+            pltpu.VMEM((depth, columns), jnp.bfloat16),
+            pltpu.VMEM((shards, rows, channels), jnp.bfloat16),
+            pltpu.VMEM((rows, columns), jnp.float32),
+            dma,
+            dma,
+            dma((2, shards)),
+            dma((shards,)),
+        ],
+        compiler_params=pltpu.CompilerParams(
+            collective_id=1, has_side_effects=True, vmem_limit_bytes=44 << 20
+        ),
+    )(gated, output_weight)
+
+
 def on_device(
     hidden_in, norm_gain, weight_in, filter_taps, filter_decay, skip_gain, tail_cache, output_weight
 ):
-    rows, width = hidden_in.shape
-    depth, _, channels = weight_in.shape
+    channels = weight_in.shape[2]
     taps = filter_taps.shape[1]
+    bands = banded_taps(filter_taps, filter_decay)
     normed = normalize_rows(hidden_in, norm_gain)
-    parts = width // depth
-    pieces = jnp.stack([normed[:, p * depth : (p + 1) * depth] for p in range(parts)])
-    pieces = lax.all_to_all(pieces, "ctx", 0, 0, tiled=True)
-    pieces = lax.all_gather(pieces, "tensor", axis=0)
-    pieces = pieces.transpose(1, 0, 2, 3)
-    shards = pieces.shape[1]
-    pieces = pieces.reshape(parts * shards * rows, depth)
-    planes = weight_in.transpose(1, 0, 2)
-
-    def projected(which):
-        partial = jnp.dot(pieces, planes[which], preferred_element_type=jnp.float32)
-        return lax.psum_scatter(
-            partial.astype(jnp.bfloat16), "ctx", scatter_dimension=0, tiled=True
-        )
-
-    key, value, query = (projected(which) for which in (1, 2, 0))
-    product = (key.astype(jnp.float32) * value.astype(jnp.float32)).astype(jnp.bfloat16)
+    query, product = projected(normed, weight_in.transpose(1, 0, 2))
     incoming = passed_along(product[product.shape[0] - taps :], "ctx", 1)
     leading = lax.axis_index("ctx") == 0
     tail = jnp.concatenate([jnp.zeros((1, channels), jnp.bfloat16), tail_cache], axis=0)
     before = jnp.where(leading, tail, incoming)
-    bands = banded_taps(filter_taps, filter_decay)
     gated = filtered_and_gated(query, before, product, skip_gain, bands)
-    totals = jnp.dot(
-        lax.all_gather(gated, "tensor", axis=1, tiled=True),
-        output_weight,
-        preferred_element_type=jnp.float32,
-    )
-    return totals.astype(jnp.bfloat16)
+    return output_projection(gated, output_weight)
 
 
 def solution(mesh):

time: 293 us -> 172 us (0.59)
  waiting for transfers between devices: 196 us -> 0.01 us
  Pallas kernels: 12.8 us -> 161 us
  matrix products: 38.4 us -> 0 us
  blocking collectives: 18.6 us -> 0 us
  between operations: 13.3 us -> 0.13 us
    pallas_call x0 -> x2, Pallas kernels: none -> 148 us  [the longest x1 99.9 us: projected(): pl.pallas_call(functools.partial(project_kernel, shards, parts), out_shap...]
    all_gather x2 -> x0, waiting for transfers between devices: 128 us -> none  [the longest x1 81.7 us: on_device(): pieces = lax.all_gather(pieces, 'tensor', axis=0)]
    reduce_scatter x3 -> x0, waiting for transfers between devices: 68.6 us -> none  [projected(): lax.psum_scatter(partial.astype(jnp.bfloat16), 'ctx', scatter_dimension=0...]
    dot_general x4 -> x0, matrix products: 38.4 us -> none  [the longest x3 26.5 us: projected(): partial = jnp.dot(pieces, planes[which], preferred_element_type=jnp.float32)]
    all_to_all x1 -> x0, blocking collectives: 18.6 us -> none  [on_device(): pieces = lax.all_to_all(pieces, 'ctx', 0, 0, tiled=True)]
  transfers between devices with their start and end apart: 6 -> 1, of which waited for: 5 -> 0; matrix products, arithmetic and copies ran while one was open for 7% -> 1% of each run, Pallas kernels for 2% -> 3%
where the time goes in v2:
time: 172 us
  Pallas kernels  161 us (94%)
  other arithmetic  4.67 us (3%)
  local copies, waits for them, and re-layouts  3.17 us (2%)
  starting transfers between devices  3.14 us (2%)
    pallas_call x1, Pallas kernels, projected(): pl.pallas_call(functools.partial(project_kernel, shards, parts), out_shap...  99.9 us
    pallas_call x1, Pallas kernels, output_projection(): pl.pallas_call(functools.partial(output_kernel, shards), out_shape=jax.Sh...  47.9 us
    pallas_call x1, Pallas kernels, filtered_and_gated(): pl.pallas_call(filter_kernel, grid=(channels // LANES,), in_specs=[pl.Blo...  7.41 us
    pallas_call x1, Pallas kernels, banded_taps(): pl.pallas_call(toeplitz_kernel, grid=(groups // block,), in_specs=[pl.Blo...  5.49 us
  transfers between devices with their start and end apart: 1, of which 0 were waited for; matrix products, arithmetic and copies ran while one was open for 1% of the time, Pallas kernels for 3%

profile of v2, /device:TPU:0, one launch (start us, length us, event | category | flops | bytes accessed | tf_op | source)
XLA Modules:
  0.0 171.8 jit_solution(4053721514848919080)
XLA Ops:
  0.0 1.5 fusion
  1.5 1.5 fusion.2.normed_ref
  3.1 0.0 copy-start.5
  3.1 0.0 copy-start.4
  3.1 99.9 %shard_map.82 = (f32[256,1024]{1,0:T(8,128)S(1)}, bf16[256,1024]{1,0:T(8,128)(2,1)S(1)}) custom-call(bf16[64,8192]{1,0:T(8,128)(2,1)S(1)} %fusion.2.normed_ref, bf16[3,2048,1024]{2,1,0:T(8,128)(2,1)} %bitcast.3), custom_call_target="tpu_custom_call" | custom-call | tf_op jit(solution)/shard_map/pallas_call | solution.py:312
  103.0 0.0 copy-start.2
  103.0 1.0 copy-done.2
  103.9 0.0 copy-start.1
  104.0 3.1 %collective-permute-start = (bf16[128,1024]{1,0:T(8,128)(2,1)S(1)}, bf16[128,1024]{1,0:T(8,128)(2,1)S(1)}, u32[]{:S(2)}, u32[]{:S(2)}) collective-permute-start(bf16[128,1024]{1,0:T(8,128)(2,1)S(1)} %slice.3), channel_id=1, source_target_pairs={{0,1},{1,2},{2,3},{4,5},{5,6},{6,7},{8,9},{9,10},{10,11},{12,13},{... | collective-permute-start | bytes 786440 | tf_op jit(solution)/shard_map/ppermute | solution.py:16
  107.1 0.0 copy-done.5
  107.2 0.0 copy-done.4
  107.2 0.1 exponential_multiply_fusion
  107.3 0.1 pad.3.clone
  107.3 0.1 rev.3
  107.4 0.7 maximum_maximum_fusion.rows_ref
  108.1 0.0 copy-start.3
  108.1 5.5 %shard_map.83.bands_ref = bf16[64,128,256]{2,1,0:T(8,128)(2,1)} custom-call(f32[64,256]{1,0:T(8,128)} %maximum_maximum_fusion.rows_ref), custom_call_target="tpu_custom_call" | custom-call | flops 16777216 | bytes 4194304 | tf_op jit(solution)/shard_map/pallas_call | solution.py:44
  113.6 0.0 copy-done.1
  113.6 0.0 collective-permute-done
  113.6 0.0 copy-done.3
  113.6 0.8 pad_select_fusion.before_ref
  114.4 7.4 %shard_map.84.gated_ref = bf16[256,1024]{1,0:T(8,128)(2,1)} custom-call(f32[256,1024]{1,0:T(8,128)} %copy-done.2, bf16[128,1024]{1,0:T(8,128)(2,1)} %pad_select_fusion.before_ref, bf16[256,1024]{1,0:T(8,128)(2,1)} %copy-done.1, f32[1,1024]{1,0:T(1,128)} %bitcast.4, bf16[64,128,256]{2,1,0:T(8,128)(2,1)} %shard_map.83.bands_ref), custom_call_target="tpu_custom_call" | custom-call | tf_op jit(solution)/shard_map/pallas_call | solution.py:85
  121.8 0.0 copy-start
  121.8 1.0 copy-done
  122.9 47.9 %shard_map.85 = bf16[256,2048]{1,0:T(8,128)(2,1)S(1)} custom-call(bf16[256,1024]{1,0:T(8,128)(2,1)S(1)} %copy-done, bf16[4096,2048]{1,0:T(8,128)(2,1)} %weight_ref.1), custom_call_target="tpu_custom_call" | custom-call | tf_op jit(solution)/shard_map/pallas_call | solution.py:379
  170.8 1.0 copy.10
  (6 shorter events, 0.0 us)
Async XLA Ops:
  3.1 104.0 %copy-start.5 = (f32[64]{0:T(128)S(1)}, f32[64]{0:T(128)}, u32[]{:S(2)}) copy-start(f32[64]{0:T(128)} %param.12) | copy-start | bytes 772
  3.1 104.1 %copy-start.4 = (f32[64,128]{1,0:T(8,128)S(1)}, f32[64,128]{1,0:T(8,128)}, u32[]{:S(2)}) copy-start(f32[64,128]{1,0:T(8,128)} %param.11) | copy-start | bytes 98308
  103.0 1.0 copy-start.2
  103.9 9.7 %copy-start.1 = (bf16[256,1024]{1,0:T(8,128)(2,1)}, bf16[256,1024]{1,0:T(8,128)(2,1)S(1)}, u32[]{:S(2)}) copy-start(bf16[256,1024]{1,0:T(8,128)(2,1)S(1)} %get-tuple-element.8.product_ref) | copy-start | bytes 1572868
  104.0 9.7 %collective-permute-start = (bf16[128,1024]{1,0:T(8,128)(2,1)S(1)}, bf16[128,1024]{1,0:T(8,128)(2,1)S(1)}, u32[]{:S(2)}, u32[]{:S(2)}) collective-permute-start(bf16[128,1024]{1,0:T(8,128)(2,1)S(1)} %slice.3), channel_id=1, source_target_pairs={{0,1},{1,2},{2,3},{4,5},{5,6},{6,7},{8,9},{9,10},{10,11},{12,13},{... | collective-permute-start | bytes 786440 | tf_op jit(solution)/shard_map/ppermute | solution.py:16
  108.1 5.5 %copy-start.3 = (bf16[127,1024]{1,0:T(8,128)(2,1)S(1)}, bf16[127,1024]{1,0:T(8,128)(2,1)}, u32[]{:S(2)}) copy-start(bf16[127,1024]{1,0:T(8,128)(2,1)} %param.14) | copy-start | bytes 780292
  121.8 1.0 copy-start

commit v3 on v0

v3 whole, which is shorter than its diff:
```python
import functools

import jax
import jax.numpy as jnp
from jax import lax
from jax.experimental import pallas as pl
from jax.experimental.pallas import tpu as pltpu
from jax.sharding import PartitionSpec as P

GROUP = 16
LANES = 128
MESH = pl.DeviceIdType.MESH


def normalize_rows(hidden_in, norm_gain):
    values = hidden_in.astype(jnp.float32)
    scaled = lax.rsqrt(jnp.mean(values * values, axis=-1, keepdims=True) + 1e-06)
    return (values * scaled * norm_gain[None, :]).astype(jnp.bfloat16)


def first_rows(filter_taps, filter_decay):
    groups, tap_count = filter_taps.shape
    lags = jnp.arange(tap_count).astype(jnp.float32)
    taps_full = filter_taps * jnp.exp(-filter_decay[:, None] * lags[None, :])
    return jnp.pad(taps_full[:, ::-1], ((0, 0), (1, tap_count - 1)))


def span(index, size):
    return pl.ds(pl.multiple_of(index * size, size), size)


def greet(peers):
    barrier = pltpu.get_barrier_semaphore()
    for axis, peer, there in peers:

        @pl.when(there)
        def _(axis=axis, peer=peer):
            pl.semaphore_signal(barrier, inc=1, device_id={axis: peer}, device_id_type=MESH)

    pl.semaphore_wait(barrier, sum(jnp.where(there, 1, 0) for _, _, there in peers))


class Line:
    def __init__(self, count, pieces, view, send_sem, recv_sem):
        self.count, self.pieces, self.view = count, pieces, view
        self.send_sem, self.recv_sem = send_sem, recv_sem
        self.place = lax.axis_index("tensor")

    def inside(self, position):
        return (position >= 0) & (position < self.count)

    def hop(self, origin, piece, up):
        ref = self.view(origin, piece)
        return pltpu.make_async_remote_copy(
            src_ref=ref,
            dst_ref=ref,
            send_sem=self.send_sem.at[up, origin, piece],
            recv_sem=self.recv_sem.at[origin, piece],
            device_id={"tensor": jnp.clip(self.place + 2 * up - 1, 0, self.count - 1)},
            device_id_type=MESH,
        )

    def send(self, origin, piece, up):
        @pl.when(self.inside(self.place + 2 * up - 1))
        def _():
            self.hop(origin, piece, up).start()

    def pass_on(self, distance, piece, up):
        origin = self.place - distance * (2 * up - 1)

        @pl.when(self.inside(origin))
        def _():
            source = jnp.clip(origin, 0, self.count - 1)
            self.hop(source, piece, up).wait_recv()
            self.send(source, piece, up)

    def sent(self):
        def step(index, carry):
            origin, piece = index // self.pieces, lax.rem(index, self.pieces)

            @pl.when((origin <= self.place) & (self.place + 1 < self.count))
            def _():
                self.hop(origin, piece, 1).wait_send()

            @pl.when((origin >= self.place) & (self.place > 0))
            def _():
                self.hop(origin, piece, 0).wait_send()

            return carry

        lax.fori_loop(0, self.count * self.pieces, step, 0)


def mixer_kernel(
    shards,
    parts,
    normed_ref,
    planes_ref,
    first_ref,
    skip_ref,
    tail_ref,
    weight_ref,
    out_ref,
    planes,
    slots,
    partial,
    arrived,
    query,
    product,
    before,
    bands,
    weight,
    gated,
    total,
    load_sem,
    own_sem,
    swap_send,
    swap_recv,
    line_send,
    line_recv,
    sum_send,
    sum_recv,
    tail_send,
    tail_recv,
    gated_send,
    gated_recv,
):
    rows = normed_ref.shape[0]
    _, depth, channels = planes.shape
    groups, taps, _ = bands.shape
    chunks, all_rows, chunk = gated.shape[1:]
    columns = out_ref.shape[1]
    tile = min(256, channels)
    me, place = lax.axis_index("ctx"), lax.axis_index("tensor")
    others = [lax.rem(me + 1 + k, parts) for k in range(parts - 1)]

    loads = [
        pltpu.make_async_copy(planes_ref.at[g], planes.at[g], load_sem.at[g]) for g in (1, 2, 0)
    ]
    for load in loads:
        load.start()
    own = pltpu.make_async_copy(
        normed_ref.at[:, span(me, depth)], slots.at[place, span(me, rows)], own_sem
    )
    own.start()
    last_load = pltpu.make_async_copy(weight_ref, weight, load_sem.at[3])
    last_load.start()
    tail_load = pltpu.make_async_copy(tail_ref, before, load_sem.at[4])

    @pl.when(me == 0)
    def _():
        tail_load.start()

    neighbours = [
        ("tensor", jnp.maximum(place - 1, 0), place > 0),
        ("tensor", jnp.minimum(place + 1, shards - 1), place < shards - 1),
    ]
    greet([("ctx", other, me >= 0) for other in others] + neighbours)

    swaps = [
        pltpu.make_async_remote_copy(
            src_ref=normed_ref.at[:, span(other, depth)],
            dst_ref=slots.at[place, span(me, rows)],
            send_sem=swap_send.at[k],
            recv_sem=swap_recv.at[parts - 2 - k],
            device_id={"ctx": other},
            device_id_type=MESH,
        )
        for k, other in enumerate(others)
    ]
    for swap in swaps:
        swap.start()
    line = Line(
        shards, parts, lambda origin, c: slots.at[origin, span(c, rows)], line_send, line_recv
    )
    own.wait()
    line.send(place, me, 0)
    line.send(place, me, 1)

    for k in range(parts - 1):
        swaps[parts - 2 - k].wait_recv()
        line.send(place, others[k], 0)
        line.send(place, others[k], 1)

    def write_band(group, carry):
        row = jnp.broadcast_to(first_ref[pl.ds(group, 1), :], (taps, 2 * taps))
        bands[group] = pltpu.roll(row, 0, 1, stride=1, stride_axis=0).astype(jnp.bfloat16)
        return carry

    lax.fori_loop(0, groups, write_band, 0)
    for load in loads:
        load.wait()

    tiles = channels // tile

    def project(origin, k):
        def step(index, carry):
            g, column = lax.rem(index // tiles + 1, 3), lax.rem(index, tiles)
            where = span(column, tile)
            partial[g, origin, :, where] = jnp.dot(
                slots[origin], planes[g, :, where], preferred_element_type=jnp.float32
            ).astype(jnp.bfloat16)

            @pl.when(column == tiles - 1)
            def _():
                for k, other in enumerate(others):
                    pltpu.make_async_remote_copy(
                        src_ref=partial.at[g, origin, span(other, rows)],
                        dst_ref=arrived.at[g, parts - 2 - k, span(origin, rows)],
                        send_sem=sum_send,
                        recv_sem=sum_recv.at[g],
                        device_id={"ctx": other},
                        device_id_type=MESH,
                    ).start()

            return carry

        steps = 3 * tiles
        lax.fori_loop(k * steps // parts, (k + 1) * steps // parts, step, 0)

    def project_from(distance, k):
        below, above = place - distance, place + distance

        @pl.when(line.inside(below))
        def _():
            project(jnp.maximum(below, 0), k)

        @pl.when(line.inside(above) & (distance > 0))
        def _():
            project(jnp.minimum(above, shards - 1), k)

    def stage(index, carry):
        distance, k = index // parts, lax.rem(index, parts)
        project_from(distance, k)

        @pl.when(distance + 1 < shards)
        def _():
            piece = lax.rem(me + k, parts)
            line.pass_on(distance + 1, piece, 1)
            line.pass_on(distance + 1, piece, 0)

        return carry

    lax.fori_loop(0, shards * parts, stage, 0)

    def summed(g, origin):
        value = partial[g, origin, span(me, rows)].astype(jnp.float32)
        for k in range(parts - 1):
            value = value + arrived[g, k, span(origin, rows)].astype(jnp.float32)
        return value

    for g in (1, 2):
        pltpu.make_async_copy(arrived.at[g], arrived.at[g], sum_recv.at[g]).wait()

    def write_product(step, carry):
        origin = shards - 1 - step
        product[span(origin, rows), :] = (summed(1, origin) * summed(2, origin)).astype(
            jnp.bfloat16
        )
        return carry

    tail_steps = -(-taps // rows)
    lax.fori_loop(0, tail_steps, write_product, 0)
    tail = pltpu.make_async_remote_copy(
        src_ref=product.at[pl.ds(all_rows - taps, taps)],
        dst_ref=before,
        send_sem=tail_send,
        recv_sem=tail_recv,
        device_id={"ctx": jnp.minimum(me + 1, parts - 1)},
        device_id_type=MESH,
    )

    @pl.when(me + 1 < parts)
    def _():
        tail.start()

    lax.fori_loop(tail_steps, shards, write_product, 0)
    pltpu.make_async_copy(arrived.at[0], arrived.at[0], sum_recv.at[0]).wait()

    def write_query(origin, carry):
        query[span(origin, rows), :] = summed(0, origin)
        return carry

    lax.fori_loop(0, shards, write_query, 0)

    @pl.when(me > 0)
    def _():
        tail.wait_recv()

    @pl.when(me == 0)
    def _():
        tail_load.wait()

    per, windows_count = LANES // GROUP, all_rows // taps

    def filter_lanes(block, c, offset):
        where = span(block, LANES)
        extended = jnp.concatenate([before[:, where], product[:, where]], axis=0)
        windows = jnp.concatenate(
            [extended[b * taps : (b + 2) * taps] for b in range(windows_count)], axis=1
        )
        lane = lax.broadcasted_iota(jnp.int32, windows.shape, 1)
        owner = lax.rem(lane, LANES) // GROUP
        filtered = jnp.zeros((taps, windows_count * LANES), jnp.float32)
        for group in range(per):
            mine = jnp.where(owner == group, windows, jnp.zeros_like(windows))
            filtered = filtered + jnp.dot(
                bands[block * per + group], mine, preferred_element_type=jnp.float32
            )
        for b in range(windows_count):
            inner = pl.ds(b * taps, taps)
            direct = skip_ref[:, where] * product[inner, where].astype(jnp.float32)
            gated[place, c, inner, pl.ds(offset, LANES)] = (
                query[inner, where] * (filtered[:, b * LANES : (b + 1) * LANES] + direct)
            ).astype(jnp.bfloat16)

    gated_line = Line(
        shards, chunks, lambda origin, c: gated.at[origin, c], gated_send, gated_recv
    )

    def filter_chunk(c, carry):
        for part in range(chunk // LANES):
            filter_lanes(c * (chunk // LANES) + part, c, part * LANES)
        gated_line.send(place, c, 0)
        gated_line.send(place, c, 1)
        return carry

    lax.fori_loop(0, chunks, filter_chunk, 0)
    last_load.wait()
    wide = min(512, columns)

    def multiply(origin, c, fresh):
        deep = span(origin * chunks + c, chunk)

        def column(index, carry):
            where = span(index, wide)
            value = jnp.dot(
                gated[origin, c], weight[deep, where], preferred_element_type=jnp.float32
            )
            total[:, where] = value if fresh else total[:, where] + value
            return carry

        lax.fori_loop(0, columns // wide, column, 0)

    multiply(place, 0, True)

    def multiply_own(c, carry):
        multiply(place, c, False)
        return carry

    lax.fori_loop(1, chunks, multiply_own, 0)
    first_up = jnp.where(2 * place >= shards, 1, 0)

    def collect(index, carry):
        distance, side = index // (2 * chunks) + 1, lax.rem(index // chunks, 2)
        c = lax.rem(index, chunks)
        up = lax.rem(first_up + side, 2)
        gated_line.pass_on(distance, c, up)
        origin = place - distance * (2 * up - 1)

        @pl.when(gated_line.inside(origin))
        def _():
            multiply(jnp.clip(origin, 0, shards - 1), c, False)

        return carry

    lax.fori_loop(0, 2 * chunks * (shards - 1), collect, 0)
    out_ref[...] = total[...].astype(jnp.bfloat16)

    for swap in swaps:
        swap.wait_send()

    @pl.when(me + 1 < parts)
    def _():
        tail.wait_send()

    line.sent()
    gated_line.sent()
    pltpu.make_async_copy(arrived, arrived, sum_send).wait()


def on_device(
    hidden_in, norm_gain, weight_in, filter_taps, filter_decay, skip_gain, tail_cache, output_weight
):
    shards, parts = lax.axis_size("tensor"), lax.axis_size("ctx")
    rows = hidden_in.shape[0]
    depth, _, channels = weight_in.shape
    groups, taps = filter_taps.shape
    columns = output_weight.shape[1]
    all_rows = shards * rows
    chunk = min(256, channels)
    chunks = channels // chunk
    normed = normalize_rows(hidden_in, norm_gain)
    first = first_rows(filter_taps, filter_decay)
    tail = jnp.pad(tail_cache, ((1, 0), (0, 0)))
    vmem, anywhere = pl.BlockSpec(memory_space=pltpu.VMEM), pl.BlockSpec(memory_space=pl.ANY)
    dma = pltpu.SemaphoreType.DMA
    bf16, f32 = jnp.bfloat16, jnp.float32
    return pl.pallas_call(
        functools.partial(mixer_kernel, shards, parts),
        out_shape=jax.ShapeDtypeStruct((all_rows, columns), bf16),
        in_specs=[vmem, anywhere, vmem, vmem, anywhere, anywhere],
        out_specs=vmem,
        scratch_shapes=[
            pltpu.VMEM((3, depth, channels), bf16),
            pltpu.VMEM((shards, parts * rows, depth), bf16),
            pltpu.VMEM((3, shards, parts * rows, channels), bf16),
            pltpu.VMEM((3, parts - 1, all_rows, channels), bf16),
            pltpu.VMEM((all_rows, channels), f32),
            pltpu.VMEM((all_rows, channels), bf16),
            pltpu.VMEM((taps, channels), bf16),
            pltpu.VMEM((groups, taps, 2 * taps), bf16),
            pltpu.VMEM(output_weight.shape, bf16),
            pltpu.VMEM((shards, chunks, all_rows, chunk), bf16),
            pltpu.VMEM((all_rows, columns), f32),
            dma((5,)),
            dma,
            dma((parts - 1,)),
            dma((parts - 1,)),
            dma((2, shards, parts)),
            dma((shards, parts)),
            dma,
            dma((3,)),
            dma,
            dma,
            dma((2, shards, chunks)),
            dma((shards, chunks)),
        ],
        compiler_params=pltpu.CompilerParams(
            collective_id=0, has_side_effects=True, vmem_limit_bytes=60 << 20
        ),
    )(
        normed,
        weight_in.transpose(1, 0, 2),
        first,
        skip_gain.reshape(1, channels),
        tail,
        output_weight,
    )


def solution(mesh):
    in_specs = (
        P(("prompt", "ctx", "tensor"), None),
        P(),
        P("ctx", None, "tensor"),
        P("tensor", None),
        P("tensor"),
        P("tensor"),
        P("prompt", "tensor"),
        P(None, "tensor"),
    )
    out_specs = P(("prompt", "ctx"), "tensor")
    return jax.shard_map(
        on_device, mesh=mesh, in_specs=in_specs, out_specs=out_specs, check_vma=False
    )
```

time: 510 us -> 140 us (0.27)
  waiting for transfers between devices: 357 us -> 0 us
  Pallas kernels: 0 us -> 130 us
  local copies, waits for them, and re-layouts: 78.8 us -> 4.82 us
  matrix products: 51.1 us -> 0 us
  between operations: 13.2 us -> 0.04 us
    all_gather x3 -> x0, waiting for transfers between devices: 355 us -> none  [the longest x1 294 us: on_device(): lax.all_gather(weight_in, 'ctx', axis=0, tiled=True)]
    pallas_call x0 -> x1, Pallas kernels: none -> 130 us  [on_device(): pl.pallas_call(functools.partial(mixer_kernel, shards, parts), out_shape=...]
    dot_general x3 -> x0, matrix products: 51.1 us -> none  [the longest x1 21.9 us: on_device(): jnp.einsum('td,dgc->tgc', normed, lax.all_gather(weight_in, 'ctx', axis=0...]
    reshape x2 -> x0, local copies, waits for them, and re-layouts: 35.4 us -> none  [the longest x1 32.8 us: banded_taps(): repeated[:, :shard_rows * width].reshape(group_count, shard_rows, width)]
    unnamed x11 -> x3, local copies, waits for them, and re-layouts: 22.1 us -> 2.31 us
    another operation x1 -> x0, local copies, waits for them, and re-layouts: 10.3 us -> none  [banded_taps(): repeated = jnp.tile(first_row, (1, shard_rows))]
    slice x2 -> x0, local copies, waits for them, and re-layouts: 8.69 us -> none  [the longest x1 8.62 us: banded_taps(): repeated[:, :shard_rows * width].reshape(group_count, shard_rows, width)]
  transfers between devices with their start and end apart: 4 -> 0, of which waited for: 4 -> 0; matrix products, arithmetic and copies ran while one was open for 15% -> 0% of each run, Pallas kernels for 0% -> 0%
where the time goes in v3:
time: 140 us
  Pallas kernels  130 us (93%)
  other arithmetic  5.16 us (4%)
  local copies, waits for them, and re-layouts  4.82 us (3%)
    pallas_call x1, Pallas kernels, on_device(): pl.pallas_call(functools.partial(mixer_kernel, shards, parts), out_shape=...  130 us

profile of v3, /device:TPU:0, one launch (start us, length us, event | category | flops | bytes accessed | tf_op | source)
XLA Modules:
  0.0 139.5 jit_solution(15817383804489645515)
XLA Ops:
  0.0 0.0 copy-start
  0.0 0.7 neg.4
  0.7 1.5 %fusion = f32[64]{0:T(128)S(1)} fusion(bf16[64,8192]{1,0:T(8,128)(2,1)} %param.8), kind=kLoop, calls=%fused_computation.2 | loop fusion | flops 1572800 | bytes 1048832 | tf_op jit(solution)/shard_map/reduce_sum | solution.py:17
  2.3 0.8 exponential_multiply_fusion
  3.2 0.1 rev.3
  3.2 0.7 pad.8.first_ref
  3.9 1.7 %pad.9.tail_ref = bf16[128,1024]{1,0:T(8,128)(2,1)} pad(bf16[127,1024]{1,0:T(8,128)(2,1)} %param.14, bf16[]{:T(256)} %constant.10.clone.1), padding=1_0x0_0 | pad | bytes 522242 | tf_op jit(solution)/shard_map/jit(_pad)/pad | solution.py:395
  5.7 0.0 copy-done
  5.7 2.0 %fusion.2.normed_ref = bf16[64,8192]{1,0:T(8,128)(2,1)} fusion(bf16[64,8192]{1,0:T(8,128)(2,1)S(1)} %copy-done, f32[8192]{0:T(1024)} %param.9, f32[64]{0:T(128)S(1)} %add_rsqrt_fusion), kind=kLoop, calls=%fused_computation.4 | loop fusion | flops 2097152 | bytes 2130176 | tf_op jit(solution)/shard_map/convert_element_type | solution.py:18
  7.7 129.5 %shard_map.82 = bf16[256,2048]{1,0:T(8,128)(2,1)} custom-call(bf16[64,8192]{1,0:T(8,128)(2,1)} %fusion.2.normed_ref, bf16[3,2048,1024]{2,1,0:T(8,128)(2,1)} %bitcast.2, f32[64,256]{1,0:T(8,128)} %pad.8.first_ref, f32[1,1024]{1,0:T(1,128)} %bitcast.3, bf16[128,1024]{1,0:T(8,128)(2,1)} %pad.9.tail_ref, bf16[4096,2048]{1,0:T(8,128)(2,1)} %weight_ref.1), custom_call_target="tpu_custom_call" | custom-call | tf_op jit(solution)/shard_map/pallas_call | solution.py:399
  137.2 2.3 %copy.10 = bf16[256,2048]{1,0:T(8,128)(2,1)} copy(bf16[256,2048]{1,0:T(8,128)(2,1)} %shard_map.82) | data formatting | bytes 2097152
  (2 shorter events, 0.0 us)
Async XLA Ops:
  0.0 5.7 %copy-start = (bf16[64,8192]{1,0:T(8,128)(2,1)S(1)}, bf16[64,8192]{1,0:T(8,128)(2,1)}, u32[]{:S(2)}) copy-start(bf16[64,8192]{1,0:T(8,128)(2,1)} %param.8) | copy-start | bytes 3145732
